TPU v7x, 512 devices: a whole 4x8x8 slice. The times are simulated.
512 devices in a mesh: sec: 4 (over x), seq: 64 (over z, y), tp: 2 (over core).
Axes of the slice: x: 4, y: 8, z: 8, core: 2. Of those that a mesh axis runs over, the one named last changes fastest.
Arguments:
- hidden: bfloat16 [16384, 5120], P('seq', ('sec', 'tp')), may hold values from -6 to 6
- projection: bfloat16 [5120, 5120], P('seq', ('sec', 'tp')), may hold values from -0.078125 to 0.078125
- norm_gain: float32 [5120], replicated, may hold values from 0.1 to 1.9
- old_logp: float32 [16384], P('seq'), may hold values from -2.5 to 0
- ref_logp: float32 [16384], P('seq'), may hold values from -2.5 to 0
- lengths: int32 [256], P('seq'), may hold values from 1 to 64, 8192 in all
- group_of: int32 [256], P('seq'), may hold values from 0 to 31, as said below
- rewards: int32 [256], P('seq'), may hold values from 0 to 4
Outputs:
- ref_states: bfloat16 [8192, 5120], P('seq', ('sec', 'tp'))
- token_terms: bfloat16 [8192, 2], P('seq')
Inputs may be any that keep to these rules, and one draw needn't show every extreme that they name: `group_of`: each group number names exactly 8 responses. The lengths sum to 8192; the longest is exactly 64.
All inputs are finite; a program needn't handle non-finite values. No bound on the sum of `lengths` on one device may be relied on, other than what follows from the above.
Results may differ from a plain program's by a relative error of at most 0.0039.
Values may be sent and summed in bfloat16 or wider, within the bound.
A program may use at most 64 MiB of HBM per device.

v0:
```python
import jax
import jax.numpy as jnp
from jax import lax
from jax.sharding import PartitionSpec as P

D = 5120
TOK_DEV = 128
RESP_DEV = 4
GROUP = 8
LMAX = 64
SLOTS = 256


def from_everyone(shard, axis):
    copies = jnp.broadcast_to(shard, (lax.axis_size(axis), *shard.shape))
    return lax.all_to_all(copies, axis, split_axis=0, concat_axis=0, tiled=True)


def joined_along(parts, dim):
    shape = list(parts.shape[1:])
    shape[dim] *= parts.shape[0]
    return jnp.moveaxis(parts, 0, dim).reshape(shape)


def gathered_copies(shard, axis, dim):
    parts = from_everyone(shard, axis)
    return joined_along(parts, dim)


def of_everyone(shard, axis):
    everything = from_everyone(shard, axis)
    return jnp.sum(everything, axis=0)


def packed_total(arrays, axis):
    ends = [0]
    for a in arrays:
        ends.append(ends[-1] + a.size)
    running = of_everyone(jnp.concatenate([a.ravel() for a in arrays]), axis)
    return tuple((running[b:e].reshape(a.shape) for a, b, e in zip(arrays, ends, ends[1:])))


def refine(input_rows, projection, norm_gain):
    widened = input_rows.astype(jnp.float32)
    full_rows = gathered_copies(input_rows, ("sec", "tp"), 1).astype(jnp.float32)
    squares = jnp.sum(full_rows * full_rows, axis=1, keepdims=True)
    normed = (full_rows * lax.rsqrt(squares / D + 1e-06) * norm_gain).astype(jnp.bfloat16)
    mixing = jnp.dot(
        normed,
        lax.all_gather(projection, "seq", axis=0, tiled=True),
        preferred_element_type=jnp.float32,
    )
    return (widened + mixing).astype(jnp.bfloat16)


def deliver(
    input_rows, token_terms, lengths, first_index, own_total, starts, seq_index, tile_rows, n_seq
):
    slot_count = input_rows.shape[0]
    slot_index = jnp.arange(slot_count, dtype=jnp.int32)
    offset = jnp.mod(slot_index - first_index, slot_count)
    filled = offset < own_total
    finish = jnp.cumsum(lengths)
    response = jnp.sum((finish[None, :] <= offset[:, None]).astype(jnp.int32), axis=1)
    response = jnp.minimum(response, lengths.shape[0] - 1)
    opening = jnp.take(finish - lengths, response)
    source = jnp.where(filled, response * LMAX + offset - opening, 0)
    send_rows = jnp.where(
        filled[:, None], jnp.take(input_rows, source, axis=0), jnp.zeros((), input_rows.dtype)
    )
    send_terms = jnp.where(
        filled[:, None], jnp.take(token_terms, source, axis=0), jnp.zeros((), token_terms.dtype)
    )
    arrived, arrived_terms = (
        lax.all_to_all(
            send_rows.reshape(n_seq, tile_rows, -1), "seq", split_axis=0, concat_axis=0, tiled=True
        ),
        lax.all_to_all(
            send_terms.reshape(n_seq, tile_rows, 2), "seq", split_axis=0, concat_axis=0, tiled=True
        ),
    )
    learner_row = jnp.arange(TOK_DEV, dtype=jnp.int32)
    packed = learner_row // tile_rows * slot_count + seq_index * tile_rows + learner_row % tile_rows
    sender = jnp.sum((starts[None, :] <= packed[:, None]).astype(jnp.int32), axis=1) - 1
    pick_index = sender * tile_rows + learner_row % tile_rows
    states = jnp.take(arrived.reshape(slot_count, -1), pick_index, axis=0)
    moved_terms = jnp.take(arrived_terms.reshape(slot_count, 2), pick_index, axis=0)
    return (states, moved_terms)


def shards(hidden, projection, norm_gain, old_logp, ref_logp, lengths, group_of, rewards):
    n_seq = lax.axis_size("seq")
    seq_index = lax.axis_index("seq")
    tile_rows = SLOTS // n_seq
    group_count = RESP_DEV * n_seq // GROUP
    member_table = (group_of[:, None] == jnp.arange(group_count, dtype=jnp.int32)[None, :]).astype(
        jnp.float32
    )
    reward_value = rewards.astype(jnp.float32)
    partial_value = jnp.stack(
        [
            jnp.dot(reward_value, member_table, precision=lax.Precision.HIGHEST),
            jnp.dot(reward_value * reward_value, member_table, precision=lax.Precision.HIGHEST),
        ]
    )
    own_total = jnp.sum(lengths)
    marker = jnp.where(jnp.arange(n_seq) == seq_index, own_total.astype(jnp.float32), 0.0)
    group_sums, found_counts = packed_total((partial_value, marker), "seq")
    counts = found_counts.astype(jnp.int32)
    group_mean = group_sums[0] / GROUP
    spread = jnp.maximum(jnp.sqrt(group_sums[1] / GROUP - group_mean * group_mean), 1.0)
    advantage = (
        reward_value - jnp.dot(member_table, group_mean, precision=lax.Precision.HIGHEST)
    ) / jnp.dot(member_table, spread, precision=lax.Precision.HIGHEST)
    log_ratio = ref_logp - old_logp
    penalty = jnp.exp(log_ratio) - log_ratio - 1.0
    token_terms = jnp.stack([jnp.repeat(advantage, LMAX), penalty], axis=1).astype(jnp.bfloat16)
    starts = jnp.cumsum(counts) - counts
    first_index = jnp.take(starts, seq_index)
    states, moved_terms = deliver(
        hidden, token_terms, lengths, first_index, own_total, starts, seq_index, tile_rows, n_seq
    )
    return (refine(states, projection, norm_gain), moved_terms)


def solution(mesh):
    in_specs = (
        P("seq", ("sec", "tp")),
        P("seq", ("sec", "tp")),
        P(),
        P("seq"),
        P("seq"),
        P("seq"),
        P("seq"),
        P("seq"),
    )
    out_specs = (P("seq", ("sec", "tp")), P("seq", None))
    return jax.shard_map(shards, mesh=mesh, in_specs=in_specs, out_specs=out_specs, check_vma=False)
```

profile of v0, /device:TPU:1, one launch (start us, length us, event | category | flops | bytes accessed | tf_op | source)
XLA Modules:
  0.0 126.8 jit_solution(15586512367325929775)
XLA Ops:
  7.9 0.8 reduce-window.18
  8.7 1.3 %fusion.37 = (s32[]{:T(128)}, s32[4]{0:T(128)S(1)}) fusion(s32[4]{0:T(128)} %param.13, s32[4,1]{0,1:T(1,128)S(1)} %reduce-window.18), kind=kLoop, calls=%fused_computation.99 | loop fusion | flops 7 | bytes 52 | tf_op jit(solution)/shard_map/reduce_sum | solution.py:106
  10.7 0.9 fusion.8
  11.6 0.9 fusion.9
  13.2 17.1 %all-to-all-start = ((f32[64,1,128]{2,1,0:T(1,128)}), f32[64,1,128]{2,1,0:T(1,128)S(1)}, u32[]{:S(2)}, u32[]{:S(2)}) async-start(f32[64,1,128]{2,1,0:T(1,128)} %broadcast_in_dim.107), calls=%async_computation | async-start | bytes 65536 | tf_op jit(solution)/shard_map/all_to_all | solution.py:16
  30.4 0.7 fusion.11
  31.8 9.4 %all-to-all-done = f32[64,1,128]{2,1,0:T(1,128)S(1)} async-done(((f32[64,1,128]{2,1,0:T(1,128)}), f32[64,1,128]{2,1,0:T(1,128)S(1)}, u32[]{:S(2)}, u32[]{:S(2)}) %all-to-all-start) | async-done | bytes 32800 | tf_op jit(solution)/shard_map/all_to_all | solution.py:16
  43.6 3.1 %fusion.36 = (s32[256]{0:T(256)S(1)}, s32[256,1]{0,1:T(1,128)S(1)}) fusion(s32[]{:T(128)} %broadcast.526, s32[]{:T(128)} %bitcast.14, s32[]{:T(128)} %bitcast.13, s32[]{:T(128)} %bitcast.12, s32[]{:T(128)} %bitcast.11, s32[256,1]{0,1:T(1,128)S(1)} %bitcast.60), kind=kLoop, calls=%fused_computation.98 | loop fusion | flops 2304 | bytes 3092 | tf_op jit(solution)/shard_map/jit(_take)/gather | solution.py:66
  47.4 1.2 gather_fusion
  49.5 1.1 select_select_fusion
  50.6 4.6 %all-to-all-start.1 = ((bf16[64,4,640]{2,1,0:T(4,128)(2,1)}), bf16[64,4,640]{2,1,0:T(4,128)(2,1)S(1)}, u32[]{:S(2)}, u32[]{:S(2)}) async-start(bf16[64,4,640]{2,1,0:T(4,128)(2,1)} %select_select_fusion), calls=%async_computation.1 | async-start | bytes 655360 | tf_op jit(solution)/shard_map/all_to_all | solution.py:75
  56.1 0.9 gather_fusion.2
  57.4 0.7 broadcast_select_fusion.2
  58.2 10.2 %all-to-all-done.1 = bf16[64,4,640]{2,1,0:T(4,128)(2,1)S(1)} async-done(((bf16[64,4,640]{2,1,0:T(4,128)(2,1)}), bf16[64,4,640]{2,1,0:T(4,128)(2,1)S(1)}, u32[]{:S(2)}, u32[]{:S(2)}) %all-to-all-start.1) | async-done | bytes 327712 | tf_op jit(solution)/shard_map/all_to_all | solution.py:75
  68.3 6.4 %all-to-all-start.3 = ((bf16[64,4,2]{1,2,0:T(2,128)(2,1)}), bf16[64,4,2]{1,2,0:T(2,128)(2,1)S(1)}, u32[]{:S(2)}, u32[]{:S(2)}) async-start(bf16[64,4,2]{1,2,0:T(2,128)(2,1)} %broadcast_select_fusion.2), calls=%async_computation.3 | async-start | bytes 65536 | tf_op jit(solution)/shard_map/all_to_all | solution.py:78
  74.9 0.9 gather_fusion.1
  76.0 9.5 %all-to-all-done.3 = bf16[64,4,2]{1,2,0:T(2,128)(2,1)S(1)} async-done(((bf16[64,4,2]{1,2,0:T(2,128)(2,1)}), bf16[64,4,2]{1,2,0:T(2,128)(2,1)S(1)}, u32[]{:S(2)}, u32[]{:S(2)}) %all-to-all-start.3) | async-done | bytes 1056 | tf_op jit(solution)/shard_map/all_to_all | solution.py:78
  85.5 1.2 broadcast_in_dim.117
  86.8 7.5 %all-to-all-start.2 = ((bf16[8,128,640]{1,2,0:T(8,128)(2,1)}), bf16[8,128,640]{1,2,0:T(8,128)(2,1)S(1)}, u32[]{:S(2)}, u32[]{:S(2)}) async-start(bf16[8,128,640]{1,2,0:T(8,128)(2,1)} %broadcast_in_dim.117), calls=%async_computation.2 | async-start | bytes 2621440 | tf_op jit(solution)/shard_map/all_to_all | solution.py:16
  94.8 0.7 gather_fusion.3
  96.2 16.0 %all-to-all-done.2 = bf16[8,128,640]{1,2,0:T(8,128)(2,1)S(1)} async-done(((bf16[8,128,640]{1,2,0:T(8,128)(2,1)}), bf16[8,128,640]{1,2,0:T(8,128)(2,1)S(1)}, u32[]{:S(2)}, u32[]{:S(2)}) %all-to-all-start.2) | async-done | bytes 1310752 | tf_op jit(solution)/shard_map/all_to_all | solution.py:16
  112.2 0.7 multiply_reduce_fusion
  112.9 2.2 %fusion.1 = bf16[128,5120]{0,1:T(8,128)(2,1)S(1)} fusion(f32[5120]{0:T(1024)S(1)} %copy-done.1, f32[128]{0:T(128)S(1)} %add_rsqrt_fusion, bf16[8,128,640]{1,2,0:T(8,128)(2,1)S(1)} %all-to-all-done.2), kind=kLoop, calls=%fused_computation.6 | loop fusion | flops 2621440 | bytes 2642432 | tf_op jit(solution)/shard_map/convert_element_type | solution.py:47
  115.2 4.8 %fusion.2 = bf16[128,640]{1,0:T(8,128)(2,1)} fusion(bf16[128,5120]{0,1:T(8,128)(2,1)S(1)} %fusion.1, bf16[5120,640]{1,0:T(8,128)(2,1)} %all-gather.2.cloned.1.call-done, bf16[128,640]{1,0:T(8,128)(2,1)S(1)} %broadcast_select_fusion), kind=kOutput, calls=%fused_computation.9 | convolution fusion | flops 839106560 | bytes 8192000 | tf_op jit(solution)/shard_map/dot_general | solution.py:48
  (54 shorter events, 8.4 us)
Async XLA Ops:
  7.2 40.3 %copy-start = (bf16[256,640]{1,0:T(8,128)(2,1)S(1)}, bf16[256,640]{1,0:T(8,128)(2,1)}, u32[]{:S(2)}) copy-start(bf16[256,640]{1,0:T(8,128)(2,1)} %param.8) | copy-start | bytes 983044
  7.2 108.0 %all-gather.2.cloned.1.call-start = ((), (), s32[]{:S(2)}) async-start(), calls=%async_computation.4 | async-start | bytes 6656000 | tf_op jit(solution)/shard_map/all_gather | solution.py:50
  13.2 27.9 %all-to-all-start = ((f32[64,1,128]{2,1,0:T(1,128)}), f32[64,1,128]{2,1,0:T(1,128)S(1)}, u32[]{:S(2)}, u32[]{:S(2)}) async-start(f32[64,1,128]{2,1,0:T(1,128)} %broadcast_in_dim.107), calls=%async_computation | async-start | bytes 65536 | tf_op jit(solution)/shard_map/all_to_all | solution.py:16
  41.4 13.9 %copy-start.2 = (s32[4]{0:T(128)S(1)}, s32[4]{0:T(128)}, u32[]{:S(2)}) copy-start(s32[4]{0:T(128)} %param.14) | copy-start | bytes 52
  41.5 14.0 %copy-start.3 = (s32[4]{0:T(128)S(1)}, s32[4]{0:T(128)}, u32[]{:S(2)}) copy-start(s32[4]{0:T(128)} %param.15) | copy-start | bytes 52
  50.6 17.7 %all-to-all-start.1 = ((bf16[64,4,640]{2,1,0:T(4,128)(2,1)}), bf16[64,4,640]{2,1,0:T(4,128)(2,1)S(1)}, u32[]{:S(2)}, u32[]{:S(2)}) async-start(bf16[64,4,640]{2,1,0:T(4,128)(2,1)} %select_select_fusion), calls=%async_computation.1 | async-start | bytes 655360 | tf_op jit(solution)/shard_map/all_to_all | solution.py:75
  68.3 17.2 %all-to-all-start.3 = ((bf16[64,4,2]{1,2,0:T(2,128)(2,1)}), bf16[64,4,2]{1,2,0:T(2,128)(2,1)S(1)}, u32[]{:S(2)}, u32[]{:S(2)}) async-start(bf16[64,4,2]{1,2,0:T(2,128)(2,1)} %broadcast_select_fusion.2), calls=%async_computation.3 | async-start | bytes 65536 | tf_op jit(solution)/shard_map/all_to_all | solution.py:78
  76.0 36.9 %copy-start.1 = (f32[5120]{0:T(1024)S(1)}, f32[5120]{0:T(1024)}, u32[]{:S(2)}) copy-start(f32[5120]{0:T(1024)} %param.10) | copy-start | bytes 61444
  86.8 25.5 %all-to-all-start.2 = ((bf16[8,128,640]{1,2,0:T(8,128)(2,1)}), bf16[8,128,640]{1,2,0:T(8,128)(2,1)S(1)}, u32[]{:S(2)}, u32[]{:S(2)}) async-start(bf16[8,128,640]{1,2,0:T(8,128)(2,1)} %broadcast_in_dim.117), calls=%async_computation.2 | async-start | bytes 2621440 | tf_op jit(solution)/shard_map/all_to_all | solution.py:16
Sparse Core Ops, SparseCore 0:
  11.0 102.4 all-gather.1
where the time goes:
time: 127 us
  waiting for transfers between devices  45.8 us (36%)
  starting transfers between devices  35.8 us (28%)
  between operations  15.5 us (12%)
  other arithmetic  12.9 us (10%)
  local copies, waits for them, and re-layouts  9.92 us (8%)
  matrix products  6.89 us (5%)
    all_to_all x2, waiting for transfers between devices, from_everyone(): return lax.all_to_all(copies, axis, split_axis=0, concat_axis=0, tiled=True)  25.4 us
    all_to_all x2, starting transfers between devices, from_everyone(): return lax.all_to_all(copies, axis, split_axis=0, concat_axis=0, tiled=True)  24.7 us
    all_to_all x1, waiting for transfers between devices, deliver(): lax.all_to_all(send_rows.reshape(n_seq, tile_rows, -1), 'seq', split_axis...  10.2 us
    all_to_all x1, waiting for transfers between devices, deliver(): lax.all_to_all(send_terms.reshape(n_seq, tile_rows, 2), 'seq', split_axis...  9.53 us
    all_to_all x1, starting transfers between devices, deliver(): lax.all_to_all(send_terms.reshape(n_seq, tile_rows, 2), 'seq', split_axis...  6.41 us
    dot_general x1, matrix products, refine(): jnp.dot(normed, lax.all_gather(projection, 'seq', axis=0, tiled=True), pr...  4.76 us
    all_to_all x1, starting transfers between devices, deliver(): lax.all_to_all(send_rows.reshape(n_seq, tile_rows, -1), 'seq', split_axis...  4.63 us
    gather x1, other arithmetic, deliver(): opening = jnp.take(finish - lengths, response)  3.12 us
  transfers between devices with their start and end apart: 5, of which 4 were waited for; matrix products, arithmetic and copies ran while one was open for 20% of the time, Pallas kernels for 0%

commit v1 on v0

v1 whole, which is shorter than its diff:
```python
import jax
import jax.numpy as jnp
from jax import lax
from jax.experimental import pallas as pl
from jax.experimental.pallas import tpu as pltpu
from jax.sharding import PartitionSpec as P

D = 5120
GROUP = 8
LMAX = 64
COLS = 640
WROWS = 80
NX, NY, NZ = 4, 8, 8
NQ = NZ // 2
TOK = 128
SLOTS = 256
TERMS = 128
WIDE = COLS + TERMS
CUT = 384
F32 = jnp.float32
BF16 = jnp.bfloat16
MESH = pl.DeviceIdType.MESH


def iota(shape, dim):
    return lax.broadcasted_iota(jnp.int32, shape, dim)


def one_hot(mask):
    return jnp.where(mask, 1.0, 0.0).astype(BF16)


def picked(table, rows):
    return jnp.dot(table, rows, preferred_element_type=F32).astype(BF16)


def kernel(
    hidden,
    shard,
    gain,
    old_logp,
    ref_logp,
    lengths,
    group_of,
    rewards,
    states_out,
    terms_out,
    info_own,
    info_y,
    info_line,
    info_z,
    send1,
    recv1,
    send2,
    recv2,
    full_rows,
    term_pair,
    weights,
    scaled,
    product,
    give,
    take,
    squares_own,
    squares_other,
    info_ys,
    info_yr,
    info_zs,
    info_zr,
    del_s,
    del_r,
    a1_s,
    a1_r,
    a2_s,
    a2_r,
    b1_s,
    b1_r,
    b2_s,
    b2_r,
    x_s,
    x_r,
    c_s,
    c_r,
    o_s,
    o_r,
):
    x = lax.axis_index("sec")
    s = lax.axis_index("seq")
    core = lax.axis_index("tp")
    y = s % NY
    z = s // NY
    half = z % 2
    q = z // 2
    other = 1 - core

    def at(x_=None, y_=None, z_=None, core_=None):
        zz = z if z_ is None else z_
        yy = y if y_ is None else y_
        return {
            "sec": x if x_ is None else x_,
            "seq": zz * NY + yy,
            "tp": core if core_ is None else core_,
        }

    pending = []

    def remote(src, dst, ssem, rsem, dev):
        return pltpu.make_async_remote_copy(
            src_ref=src, dst_ref=dst, send_sem=ssem, recv_sem=rsem, device_id=dev, device_id_type=MESH
        )

    def send(src, dst, ssem, rsem, dev):
        copy = remote(src, dst, ssem, rsem, dev)
        copy.start()
        pending.append(copy)

    def arrived(dst, ssem, rsem):
        remote(dst, dst, ssem, rsem, at(core_=other)).wait_recv()

    barrier = pltpu.get_barrier_semaphore()
    partners = [at(y_=(y + k) % NY) for k in range(1, NY)]
    partners += [at(z_=(z + k) % NZ) for k in range(1, NZ)]
    partners += [at(z_=(z + k) % NZ, core_=other) for k in range(NZ)]
    partners += [at(x_=(x + k) % NX) for k in range(1, NX)]
    for dev in partners:
        pl.semaphore_signal(barrier, inc=1, device_id=dev, device_id_type=MESH)

    lane = iota((8, 128), 1)
    length = [lengths[i] for i in range(4)]
    group = [group_of[i] for i in range(4)]
    reward = [rewards[i].astype(F32) for i in range(4)]
    opening = [0 * length[0]]
    for i in range(3):
        opening.append(opening[-1] + length[i])
    own_total = opening[3] + length[3]
    info = jnp.where(lane == s, own_total.astype(F32), 0.0)
    for i in range(4):
        info += jnp.where(lane == 64 + group[i], reward[i], 0.0)
        info += jnp.where(lane == 96 + group[i], reward[i] * reward[i], 0.0)
    info_own[...] = info
    w_rows = pl.ds(pl.multiple_of(y * WROWS, 16), WROWS)
    weights[q, w_rows, :] = shard[...]

    pl.semaphore_wait(barrier, len(partners))

    def wrow(yy):
        return pl.ds(pl.multiple_of(yy * WROWS, 16), WROWS)

    def wa(qq, yy):
        return weights.at[qq, wrow(yy), pl.ds(0, CUT)]

    def wb(qq, yy):
        return weights.at[qq, wrow(yy), pl.ds(CUT, COLS - CUT)]

    y_up, y_dn = at(y_=(y + 1) % NY), at(y_=(y + NY - 1) % NY)
    z_up, z_dn = at(z_=(z + 2) % NZ), at(z_=(z + NZ - 2) % NZ)

    for k in range(1, NY):
        send(info_own, info_y.at[k], info_ys.at[k], info_yr.at[k], at(y_=(y + k) % NY))

    own_a = shard.at[:, pl.ds(0, CUT)]
    own_b = shard.at[:, pl.ds(CUT, COLS - CUT)]
    for k in (1, 3, 2):
        send(own_a, wa(q, y), a1_s.at[k], a1_r.at[k], at(z_=(z + 2 * k) % NZ))
    send(own_a, wa(q, y), a2_s.at[0, 1, 0], a2_r.at[0, 1, 0], y_up)
    send(own_a, wa(q, y), a2_s.at[1, 1, 0], a2_r.at[1, 1, 0], y_dn)
    for k in (1, 7, 2, 6, 3, 5, 4):
        send(own_b, wb(q, y), b1_s.at[k], b1_r.at[k], at(y_=(y + k) % NY))
    send(own_b, wb(q, y), b2_s.at[0, 1, 0], b2_r.at[0, 1, 0], z_up)
    send(own_b, wb(q, y), b2_s.at[1, 1, 0], b2_r.at[1, 1, 0], z_dn)

    line = info
    for k in range(1, NY):
        arrived(info_y.at[k], info_ys.at[k], info_yr.at[k])
        line += info_y[k]
    info_line[...] = line
    for k in range(1, NZ):
        send(info_line, info_z.at[k], info_zs.at[k], info_zr.at[k], at(z_=(z + k) % NZ))

    for k in (1, 3, 2):
        qq = (q + NQ - k) % NQ
        piece = wa(qq, y)
        arrived(piece, a1_s.at[k], a1_r.at[k])
        j = NQ - k
        send(piece, piece, a2_s.at[0, 1, j], a2_r.at[0, 1, j], y_up)
        send(piece, piece, a2_s.at[1, 1, j], a2_r.at[1, 1, j], y_dn)
    for k in (1, 7, 2, 6, 3, 5, 4):
        yy = (y + NY - k) % NY
        piece = wb(q, yy)
        arrived(piece, b1_s.at[k], b1_r.at[k])
        j = NY - k
        send(piece, piece, b2_s.at[0, 1, j], b2_r.at[0, 1, j], z_up)
        send(piece, piece, b2_s.at[1, 1, j], b2_r.at[1, 1, j], z_dn)

    def forward_a(d):
        for j in (0, 3, 1, 2):
            qq = (q + j) % NQ
            for way, dev in ((0, y_up), (1, y_dn)):
                if d == 4 and (j < 2) != (way == 0):
                    continue
                yy = (y + NY - d) % NY if way == 0 else (y + d) % NY
                piece = wa(qq, yy)
                arrived(piece, a2_s.at[way, d, j], a2_r.at[way, d, j])
                if d < 3 or (d == 3 and (j < 2) == (way == 0)):
                    send(piece, piece, a2_s.at[way, d + 1, j], a2_r.at[way, d + 1, j], dev)

    def forward_b(d):
        for j in (0, 7, 1, 6, 2, 5, 3, 4):
            yy = (y + j) % NY
            for way, dev in ((0, z_up), (1, z_dn)):
                mine = (j < 4) == (way == 0)
                if d == 2 and not mine:
                    continue
                qq = (q + NQ - d) % NQ if way == 0 else (q + d) % NQ
                piece = wb(qq, yy)
                arrived(piece, b2_s.at[way, d, j], b2_r.at[way, d, j])
                if d == 1 and mine:
                    send(piece, piece, b2_s.at[way, 2, j], b2_r.at[way, 2, j], dev)

    total = line
    for k in range(1, NZ):
        arrived(info_z.at[k], info_zs.at[k], info_zr.at[k])
        total += info_z[k]

    first = (jnp.sum(jnp.where(lane < s, total, 0.0)) * 0.125).astype(jnp.int32)
    col = iota((1, SLOTS), 1)
    spot = jnp.full((1, SLOTS), -1, jnp.int32)
    for i in range(4):
        p = col - i * LMAX
        spot = jnp.where((p >= 0) & (p < length[i]), opening[i] + p, spot)
    row = iota((SLOTS, 1), 0)
    turned = ((row // 4 % 8) * 8 + row // 32) * 4 + row % 4
    table1 = one_hot((((turned - first) & (SLOTS - 1))) == spot)
    table2 = one_hot((((row - first) & (SLOTS - 1))) == spot)

    mean = total * (1.0 / GROUP)
    mean_square = pltpu.roll(mean, 96, 1)
    spread = jnp.maximum(jnp.sqrt(mean_square - mean * mean), 1.0)
    adv_col = jnp.zeros((SLOTS, 1), F32)
    for i in range(4):
        value = jnp.where(lane == 64 + group[i], (reward[i] - mean) / spread, 0.0)
        adv_col = jnp.where(row // LMAX == i, jnp.sum(value) * 0.125, adv_col)
    ratio = ref_logp[...] - old_logp[...]
    penalty = jnp.exp(ratio) - ratio - 1.0
    pen_col = jnp.sum(jnp.where(row == col, penalty, 0.0), axis=1, keepdims=True)
    term_lane = iota((SLOTS, TERMS), 1)
    terms = jnp.where(term_lane == 0, adv_col, jnp.where(term_lane == 1, pen_col, 0.0)).astype(BF16)

    send1[:, :CUT] = picked(table1, hidden[:, :CUT])
    send1[:, CUT:COLS] = picked(table2, hidden[:, CUT:])
    send1[:, COLS:] = picked(table2, terms)

    lanes1, lanes2 = pl.ds(0, CUT), pl.ds(CUT, WIDE - CUT)
    zme = 2 * q + core
    aligned = half == core

    def block(i):
        return pl.ds(pl.multiple_of(i * 32, 32), 32)

    def route_y(n, src, dst, lanes):
        dst[block(y), lanes] = src[block(y), lanes]
        for k in (4, 3, 5, 2, 6, 1, 7):
            t = (y + k) % NY
            send(src.at[block(t), lanes], dst.at[block(y), lanes], del_s.at[n, k], del_r.at[n, k], at(y_=t))

    def wait_y(n, dst, lanes):
        for k in range(1, NY):
            arrived(dst.at[block((y + NY - k) % NY), lanes], del_s.at[n, k], del_r.at[n, k])

    def z_target(zt):
        return at(z_=2 * (zt // 2) + core, core_=zt % 2)

    def route_z(n, src, dst, lanes):
        for k in (4, 3, 5, 2, 6, 1, 7):
            zt = (z + k) % NZ
            send(src.at[block(zt), lanes], dst.at[block(z), lanes], del_s.at[n, k], del_r.at[n, k], z_target(zt))

        @pl.when(aligned)
        def _():
            dst[block(z), lanes] = src[block(z), lanes]

        @pl.when(jnp.logical_not(aligned))
        def _():
            remote(
                src.at[block(z), lanes], dst.at[block(z), lanes], del_s.at[n, 0], del_r.at[n, 0],
                at(z_=2 * q + core, core_=other),
            ).start()

    def wait_z(n, dst, lanes):
        for k in range(1, NZ):
            arrived(dst.at[block((zme + NZ - k) % NZ), lanes], del_s.at[n, k], del_r.at[n, k])

        @pl.when(jnp.logical_not(aligned))
        def _():
            arrived(dst.at[block(zme), lanes], del_s.at[n, 0], del_r.at[n, 0])

    def sent_z(n, src, lanes):
        @pl.when(jnp.logical_not(aligned))
        def _():
            remote(
                src.at[block(z), lanes], src.at[block(z), lanes], del_s.at[n, 0], del_r.at[n, 0],
                at(z_=2 * q + core, core_=other),
            ).wait_send()

    route_y(0, send1, recv1, lanes1)
    route_z(1, send1, recv1, lanes2)

    forward_a(1)

    wait_y(0, recv1, lanes1)
    wait_z(1, recv1, lanes2)
    inner = iota((1, SLOTS), 1)
    swap = one_hot(((row // 4 % 8) * 8 + row // 32) * 4 + row % 4 == inner)
    send2[...] = picked(swap, recv1[...])
    route_z(2, send2, recv2, lanes1)
    route_y(3, send2, recv2, lanes2)

    forward_b(1)
    forward_a(2)

    counts = total.astype(BF16)
    sender = iota((128, SLOTS), 0)
    slot = iota((128, SLOTS), 1)
    natural = slot // 4
    swapped = (natural % 8) * 8 + natural // 8
    w = iota((TOK, 1), 0)
    packed = ((w // 4) * SLOTS + (zme * NY + y) * 4 + w % 4).astype(F32)
    same = w % 4 == col % 4

    def pick_table(order):
        low = jnp.dot(counts, one_hot(sender < order), preferred_element_type=F32)[0:1]
        high = jnp.dot(counts, one_hot(sender <= order), preferred_element_type=F32)[0:1]
        return one_hot((low <= packed) & (packed < high) & same)

    pick1, pick2 = pick_table(natural), pick_table(swapped)

    wait_z(2, recv2, lanes1)
    wait_y(3, recv2, lanes2)
    mine = pl.multiple_of(core * TOK, TOK)
    theirs = pl.multiple_of(other * TOK, TOK)
    full_rows[x, pl.ds(mine, TOK), :CUT] = picked(pick1, recv2[:, :CUT])
    full_rows[x, pl.ds(mine, TOK), CUT:] = picked(pick2, recv2[:, CUT:COLS])
    term_pair[core] = picked(pick2, recv2[:, COLS:])

    H = TOK // 2
    x_up, x_dn = at(x_=(x + 1) % NX), at(x_=(x + NX - 1) % NX)
    mate = at(core_=other)
    x_l, x_r1, x_f = (x + NX - 1) % NX, (x + 1) % NX, (x + 2) % NX

    def part(xx, base, i):
        return full_rows.at[xx, pl.ds(pl.multiple_of(base + i * H, H), H), :]

    def whole(xx, base):
        return full_rows.at[xx, pl.ds(base, TOK), :]

    send(part(x, mine, 0), part(x, mine, 0), x_s.at[0, 0], x_r.at[0, 0], x_up)
    send(part(x, mine, 1), part(x, mine, 1), x_s.at[1, 1], x_r.at[1, 1], x_dn)
    send(part(x, mine, 1), part(x, mine, 1), x_s.at[0, 1], x_r.at[0, 1], x_up)
    send(part(x, mine, 0), part(x, mine, 0), x_s.at[1, 0], x_r.at[1, 0], x_dn)
    send(whole(x, mine), whole(x, mine), c_s.at[0], c_r.at[0], mate)
    send(term_pair.at[core], term_pair.at[core], c_s.at[4], c_r.at[4], mate)

    forward_a(3)

    arrived(part(x_l, mine, 0), x_s.at[0, 0], x_r.at[0, 0])
    send(part(x_l, mine, 0), part(x_l, mine, 0), x_s.at[0, 2], x_r.at[0, 2], x_up)
    arrived(part(x_r1, mine, 1), x_s.at[1, 1], x_r.at[1, 1])
    send(part(x_r1, mine, 1), part(x_r1, mine, 1), x_s.at[1, 2], x_r.at[1, 2], x_dn)
    arrived(part(x_l, mine, 1), x_s.at[0, 1], x_r.at[0, 1])
    send(whole(x_l, mine), whole(x_l, mine), c_s.at[1], c_r.at[1], mate)
    arrived(part(x_r1, mine, 0), x_s.at[1, 0], x_r.at[1, 0])
    send(whole(x_r1, mine), whole(x_r1, mine), c_s.at[2], c_r.at[2], mate)
    arrived(part(x_f, mine, 0), x_s.at[0, 2], x_r.at[0, 2])
    arrived(part(x_f, mine, 1), x_s.at[1, 2], x_r.at[1, 2])
    send(whole(x_f, mine), whole(x_f, mine), c_s.at[3], c_r.at[3], mate)

    square = jnp.zeros((2 * TOK, 128), F32)
    for n, xx in enumerate((x, x_l, x_r1, x_f)):
        arrived(whole(xx, theirs), c_s.at[n], c_r.at[n])
        wide = full_rows[xx].astype(F32)
        g = gain[:, pl.ds(pl.multiple_of((2 * xx + half) * COLS, 128), COLS)]
        scaled[xx] = (wide * g).astype(BF16)
        for t in range(COLS // 128):
            tile = wide[:, t * 128 : (t + 1) * 128]
            square += tile * tile
    squares_own[...] = lax.dot_general(
        jnp.ones((8, 128), F32), square, (((1,), (1,)), ((), ())),
        precision=lax.Precision.HIGHEST, preferred_element_type=F32,
    )
    z_mate = at(z_=z + 1 - 2 * half)
    send(squares_own, squares_other, o_s.at[0], o_r.at[0], z_mate)
    arrived(term_pair.at[other], c_s.at[4], c_r.at[4])
    terms_out[...] = term_pair[half][:, :2]

    forward_a(4)
    for lanes in (pl.ds(0, CUT), pl.ds(CUT, COLS - CUT)):
        if lanes.start == CUT:
            forward_b(2)
        acc = jnp.dot(scaled[0], weights[0, :, lanes], preferred_element_type=F32)
        for i in range(1, NX):
            acc += jnp.dot(scaled[i], weights[i, :, lanes], preferred_element_type=F32)
        product[:, lanes] = acc

    arrived(squares_other, o_s.at[0], o_r.at[0])
    both = (squares_own[...] + squares_other[...])[0:1]
    rate = lax.rsqrt(both * (1.0 / D) + 1e-6)
    scale = jnp.sum(jnp.where(row == col, rate, 0.0), axis=1, keepdims=True)
    kept = jnp.where(aligned, 1.0, 0.0)
    refined = product[...] * scale + full_rows[x].astype(F32) * kept
    product[...] = refined
    away = pl.multiple_of((1 - half) * TOK, TOK)
    home = pl.multiple_of(half * TOK, TOK)
    give[...] = product[pl.ds(away, TOK), :].astype(BF16)
    send(give, take, o_s.at[1], o_r.at[1], z_mate)
    arrived(take, o_s.at[1], o_r.at[1])
    states_out[...] = (product[pl.ds(home, TOK), :] + take[...].astype(F32)).astype(BF16)

    for copy in pending:
        copy.wait_send()
    sent_z(1, send1, lanes2)
    sent_z(2, send2, lanes1)


def shards(hidden, projection, norm_gain, old_logp, ref_logp, lengths, group_of, rewards):
    dma = pltpu.SemaphoreType.DMA
    vmem = pl.BlockSpec(memory_space=pltpu.VMEM)
    smem = pl.BlockSpec(memory_space=pltpu.SMEM)
    pairs = []
    for shape in ((8,), (8,), (4, 8), (4,), (2, 5, 4), (8,), (2, 3, 8), (2, 3), (5,), (2,)):
        pairs += [dma(shape), dma(shape)]
    return pl.pallas_call(
        kernel,
        out_shape=(
            jax.ShapeDtypeStruct((TOK, COLS), BF16),
            jax.ShapeDtypeStruct((TOK, 2), BF16),
        ),
        in_specs=[vmem] * 5 + [smem] * 3,
        out_specs=(vmem, vmem),
        scratch_shapes=[
            pltpu.VMEM((8, 128), F32),
            pltpu.VMEM((NY, 8, 128), F32),
            pltpu.VMEM((8, 128), F32),
            pltpu.VMEM((NZ, 8, 128), F32),
            pltpu.VMEM((SLOTS, WIDE), BF16),
            pltpu.VMEM((SLOTS, WIDE), BF16),
            pltpu.VMEM((SLOTS, WIDE), BF16),
            pltpu.VMEM((SLOTS, WIDE), BF16),
            pltpu.VMEM((NX, 2 * TOK, COLS), BF16),
            pltpu.VMEM((2, TOK, TERMS), BF16),
            pltpu.VMEM((NQ, COLS, COLS), BF16),
            pltpu.VMEM((NX, 2 * TOK, COLS), BF16),
            pltpu.VMEM((2 * TOK, COLS), F32),
            pltpu.VMEM((TOK, COLS), BF16),
            pltpu.VMEM((TOK, COLS), BF16),
            pltpu.VMEM((8, 2 * TOK), F32),
            pltpu.VMEM((8, 2 * TOK), F32),
        ]
        + pairs,
        compiler_params=pltpu.CompilerParams(collective_id=0, has_side_effects=True),
    )(
        hidden,
        projection,
        norm_gain.reshape(1, D),
        old_logp.reshape(1, SLOTS),
        ref_logp.reshape(1, SLOTS),
        lengths,
        group_of,
        rewards,
    )


def solution(mesh):
    in_specs = (
        P("seq", ("sec", "tp")),
        P("seq", ("sec", "tp")),
        P(),
        P("seq"),
        P("seq"),
        P("seq"),
        P("seq"),
        P("seq"),
    )
    out_specs = (P("seq", ("sec", "tp")), P("seq", None))
    return jax.shard_map(shards, mesh=mesh, in_specs=in_specs, out_specs=out_specs, check_vma=False)
```

time: 127 us -> 79 us (0.62)
  Pallas kernels: 0 us -> 75.1 us
  waiting for transfers between devices: 45.8 us -> 0 us
  starting transfers between devices: 35.8 us -> 0 us
  between operations: 15.5 us -> 0.64 us
  other arithmetic: 12.9 us -> 0 us
  local copies, waits for them, and re-layouts: 9.92 us -> 2.95 us
  matrix products: 6.89 us -> 0 us
    pallas_call x0 -> x1, Pallas kernels: none -> 75.1 us  [shards(): pl.pallas_call(kernel, out_shape=(jax.ShapeDtypeStruct((TOK, COLS), BF16)...]
    all_to_all x4 -> x0, waiting for transfers between devices: 45.1 us -> none  [the longest x2 25.4 us: from_everyone(): return lax.all_to_all(copies, axis, split_axis=0, concat_axis=0, tiled=True)]
    all_to_all x4 -> x0, starting transfers between devices: 35.7 us -> none  [the longest x2 24.7 us: from_everyone(): return lax.all_to_all(copies, axis, split_axis=0, concat_axis=0, tiled=True)]
    dot_general x5 -> x0, matrix products: 6.89 us -> none  [the longest x1 4.76 us: refine(): jnp.dot(normed, lax.all_gather(projection, 'seq', axis=0, tiled=True), pr...]
    gather x9 -> x0, local copies, waits for them, and re-layouts: 5.5 us -> none  [the longest x2 1.34 us: deliver(): jnp.take(token_terms, source, axis=0)]
    gather x3 -> x0, other arithmetic: 3.13 us -> none  [the longest x1 3.12 us: deliver(): opening = jnp.take(finish - lengths, response)]
    select_n x8 -> x0, other arithmetic: 2.65 us -> none  [the longest x1 1.09 us: deliver(): jnp.where(filled[:, None], jnp.take(input_rows, source, axis=0), jnp.zero...]
    reduce_sum x5 -> x0, other arithmetic: 2.21 us -> none  [the longest x1 1.31 us: shards(): own_total = jnp.sum(lengths)]
  transfers between devices with their start and end apart: 5 -> 0, of which waited for: 4 -> 0; matrix products, arithmetic and copies ran while one was open for 20% -> 0% of each run, Pallas kernels for 0% -> 0%
where the time goes in v1:
time: 79 us; the launch traced here: 78.7 us
  Pallas kernels  75.1 us (95%)
  local copies, waits for them, and re-layouts  2.95 us (4%)
    pallas_call x1, Pallas kernels, shards(): pl.pallas_call(kernel, out_shape=(jax.ShapeDtypeStruct((TOK, COLS), BF16)...  75.1 us
    unnamed x1, local copies, waits for them, and re-layouts  1.6 us

profile of v1, /device:TPU:1, one launch (start us, length us, event | category | flops | bytes accessed | tf_op | source)
XLA Modules:
  0.0 78.7 jit_solution(9103429052866311916)
XLA Ops:
  0.6 75.1 %shard_map.95 = (bf16[128,640]{1,0:T(8,128)(2,1)}, bf16[128,2]{1,0:T(8,128)(2,1)}) custom-call(bf16[256,640]{1,0:T(8,128)(2,1)} %hidden.1, bf16[80,640]{1,0:T(8,128)(2,1)} %shard.1, f32[1,5120]{1,0:T(1,128)} %bitcast.3, f32[1,256]{1,0:T(1,128)} %bitcast.4, f32[1,256]{1,0:T(1,128)} %bitcast.5, s32[4]{0:T(128)} %lengths.1, s32[4]{0:T(128)} %group_of.1, s32[4]{0:T(128)} %rewards.1), custom_call_target="tpu_custom_call" | custom-call | tf_op jit(solution)/shard_map/pallas_call | solution.py:430
  75.8 1.4 %copy.10 = bf16[128,2]{0,1:T(2,128)(2,1)} copy(bf16[128,2]{1,0:T(8,128)(2,1)} %get-tuple-element.3) | data formatting | bytes 1024 | tf_op jit(solution)/shard_map/pallas_call | solution.py:430
  77.1 1.6 %copy.12 = bf16[128,640]{1,0:T(8,128)(2,1)} copy(bf16[128,640]{1,0:T(8,128)(2,1)} %get-tuple-element.6) | data formatting | bytes 327680

commit v2 on v0

v2 whole, which is shorter than its diff:
```python
import jax
import jax.numpy as jnp
from jax import lax
from jax.experimental import pallas as pl
from jax.experimental.pallas import tpu as pltpu
from jax.sharding import PartitionSpec as P

D = 5120
GROUP = 8
LMAX = 64
COLS = 640
BOTH = 2 * COLS
WROWS = 80
NX, NY, NZ = 4, 8, 8
NQ = NZ // 2
TOK = 128
SLOTS = 256
TERMS = 128
CUT = 384
WIDE = COLS + TERMS
WCUT = 768
F32 = jnp.float32
BF16 = jnp.bfloat16
MESH = pl.DeviceIdType.MESH
ORDER = (
    (2, 0, 1), (2, 1, 1), (3, 1, 0, 0), (3, 1, 1, 0), (0, 0), (0, 1), (2, 0, 2), (2, 1, 2),
    (4, 1, 0, 0), (3, 2, 0, 0), (3, 2, 1, 0), (3, 1, 0, 3), (3, 1, 1, 3), (4, 1, 1, 7), (3, 1, 0, 1), (3, 1, 1, 1),
    (4, 1, 0, 1), (2, 0, 3), (2, 1, 3), (1, 0), (1, 1), (3, 3, 0, 0), (3, 2, 0, 3), (3, 2, 1, 3),
    (4, 1, 1, 6), (3, 2, 0, 1), (3, 2, 1, 1), (2, 0, 4), (2, 1, 4), (4, 1, 0, 2), (3, 1, 0, 2), (3, 1, 1, 2),
    (3, 3, 1, 3), (4, 1, 1, 5), (3, 3, 0, 1), (3, 2, 1, 2), (3, 2, 0, 2), (4, 1, 0, 3), (3, 3, 1, 2), (4, 1, 1, 4),
)


def iota(shape, dim):
    return lax.broadcasted_iota(jnp.int32, shape, dim)


def one_hot(mask):
    return jnp.where(mask, 1.0, 0.0).astype(BF16)


def picked(table, rows):
    return jnp.dot(table, rows, preferred_element_type=F32).astype(BF16)


def flat(rows):
    return rows.reshape(SLOTS, rows.shape[-1])


def tiles(rows):
    return rows.reshape(8, 32, rows.shape[-1])


class Links:
    def __init__(self):
        self.x, self.s, self.core = (lax.axis_index(n) for n in ("sec", "seq", "tp"))
        self.y, self.z = self.s % NY, self.s // NY
        self.half, self.q = self.z % 2, self.z // 2
        self.pending = []

    def at(self, x=None, y=None, z=None, core=None):
        zz = self.z if z is None else z
        yy = self.y if y is None else y
        return {
            "sec": self.x if x is None else x,
            "seq": zz * NY + yy,
            "tp": self.core if core is None else core,
        }

    def remote(self, src, dst, sems, dev):
        return pltpu.make_async_remote_copy(
            src_ref=src, dst_ref=dst, send_sem=sems[0], recv_sem=sems[1], device_id=dev, device_id_type=MESH
        )

    def send(self, src, dst, sems, dev):
        copy = self.remote(src, dst, sems, dev)
        copy.start()
        self.pending.append(copy)

    def arrived(self, dst, sems):
        self.remote(dst, dst, sems, self.at(core=1 - self.core)).wait_recv()

    def finish(self):
        for copy in self.pending:
            copy.wait_send()


def pair(sems, *index):
    return sems[0].at[index], sems[1].at[index]


def product_core(net, refs, sems):
    shard, gain, weights, scaled, raw, product, give, take, home, squares, hidden, hidden0, terms, states_out, terms_out = refs
    swap_sem, pa, pf, pb, a2, b2, r_sem, o_sem, own_sem = sems
    x, y, z, q, half = net.x, net.y, net.z, net.q, net.half
    zm = z + 1 - 2 * half
    mate = net.at(core=1)

    def rows(qq, yy):
        return pl.ds(pl.multiple_of(qq * COLS + yy * WROWS, 16), WROWS)

    def wa(qq, yy):
        return weights.at[rows(qq, yy), pl.ds(0, WCUT)]

    def wb(qq, yy):
        return weights.at[rows(qq, yy), pl.ds(WCUT, BOTH - WCUT)]

    def wa_part(qq, yy, way):
        return weights.at[rows(qq, yy), pl.ds(way * WCUT // 2, WCUT // 2)]

    def wb_part(qq, yy, way):
        return weights.at[rows(qq, yy), pl.ds(WCUT + way * (BOTH - WCUT) // 2, (BOTH - WCUT) // 2)]

    y_way = net.at(y=(y + 1) % NY), net.at(y=(y + NY - 1) % NY)
    z_way = net.at(z=(z + 2) % NZ), net.at(z=(z + NZ - 2) % NZ)

    def along_y(j):
        piece = wa((q + j) % NQ, y)
        for way in (0, 1):
            net.send(piece, piece, pair(a2, way, 1, j), y_way[way])

    def along_z(j):
        piece = wb(q, (y + j) % NY)
        for way in (0, 1):
            net.send(piece, piece, pair(b2, way, 1, j), z_way[way])

    own = pltpu.make_async_copy(shard, weights.at[rows(q, y), pl.ds(0, COLS)], own_sem.at[0])
    own.start()
    net.send(hidden, hidden0, pair(swap_sem, 0), mate)
    own.wait()
    net.arrived(weights.at[rows(q, y), pl.ds(COLS, COLS)], pair(swap_sem, 1))
    for way in (0, 1):
        net.send(wa(q, y), wa(q, y), pair(pa, way), z_way[way])
    for way in (0, 1):
        net.send(wb(q, y), wb(q, y), pair(pb, way, 1), y_way[way])
    along_y(0)
    along_z(0)

    met = []

    def first_a(way):
        qq = (q + 3 - 2 * way) % NQ
        net.arrived(wa(qq, y), pair(pa, way))
        part = wa_part(qq, y, way)
        net.send(part, part, pair(pf, way), z_way[way])
        along_y(3 - 2 * way)

    def far_a(way):
        net.arrived(wa_part((q + 2) % NQ, y, way), pair(pf, way))
        if "far" in met:
            along_y(2)
        met.append("far")

    def first_b(way, d):
        yy = (y + (d if way else NY - d)) % NY
        part = wb_part(q, yy, way)
        piece = part if d == 4 else wb(q, yy)
        net.arrived(piece, pair(pb, way, d))
        if d < 3:
            net.send(piece, piece, pair(pb, way, d + 1), y_way[way])
        elif d == 3:
            net.send(part, part, pair(pb, way, 4), y_way[way])
        if d < 4:
            along_z(d if way else NY - d)
        elif "half" in met:
            along_z(4)
        else:
            met.append("half")

    waiting = [(3, d, way, j) for d in (1, 2, 3) for way in (0, 1) for j in range(NQ)]
    waiting += [(3, 4, j // 2, j) for j in range(NQ)]
    waiting += [(4, 1, way, j) for way in (0, 1) for j in range(NY)]
    waiting += [(4, 2, j // 4, j) for j in range(NY)]

    def next_a(d, way, j):
        waiting.remove((3, d, way, j))
        piece = wa((q + j) % NQ, (y + (d if way else NY - d)) % NY)
        net.arrived(piece, pair(a2, way, d, j))
        if d < 3 or (d == 3 and j // 2 == way):
            net.send(piece, piece, pair(a2, way, d + 1, j), y_way[way])

    def next_b(d, way, j):
        waiting.remove((4, d, way, j))
        piece = wb((q + (d if way else NQ - d)) % NQ, (y + j) % NY)
        net.arrived(piece, pair(b2, way, d, j))
        if d == 1 and j // 4 == way:
            net.send(piece, piece, pair(b2, way, 2, j), z_way[way])

    hops = (first_a, far_a, first_b, next_a, next_b)
    for kind, *index in ORDER:
        hops[kind](*index)

    for n, xx in enumerate((x, (x + NX - 1) % NX, (x + 1) % NX, (x + 2) % NX)):
        for i in range(2):
            net.arrived(raw.at[xx, pl.ds(i * TOK, TOK), :], pair(r_sem, n, i))
        g = gain[:, pl.ds(pl.multiple_of((2 * xx + half) * COLS, 128), COLS)]
        scaled[:, pl.ds(pl.multiple_of(xx * COLS, 128), COLS)] = (raw[xx].astype(F32) * g).astype(BF16)
    net.arrived(terms, pair(o_sem, 5))
    terms_out[...] = terms[:, :2]
    net.arrived(squares.at[0], pair(o_sem, 0))
    net.arrived(squares.at[1], pair(o_sem, 1))
    rate = lax.rsqrt((squares[0] + squares[1])[0:1] * (1.0 / D) + 1e-6)
    scale = jnp.sum(jnp.where(iota((SLOTS, 1), 0) == iota((1, SLOTS), 1), rate, 0.0), axis=1, keepdims=True)
    away = pl.ds(pl.multiple_of((1 - half) * TOK, TOK), TOK)
    near = pl.ds(pl.multiple_of(half * TOK, TOK), TOK)

    for c, kind in ((0, 3), (1, 4)):
        for item in [w for w in waiting if w[0] == kind]:
            hops[kind](*item[1:])
        cols = pl.ds(c * COLS, COLS)
        part = jnp.dot(scaled[...], weights[:, cols], preferred_element_type=F32)
        kept = jnp.where(half == c, 1.0, 0.0)
        product[:, cols] = part * scale + raw[x].astype(F32) * kept
        give[c] = product[away, cols].astype(BF16)
        net.send(give.at[c], take, pair(o_sem, 2 + c), net.at(z=zm, core=c))
    net.send(product.at[near, pl.ds(COLS, COLS)], home, pair(o_sem, 4), mate)
    net.arrived(take, pair(o_sem, 2))
    states_out[...] = (product[near, :COLS] + take[...].astype(F32)).astype(BF16)
    net.finish()


def token_core(net, refs, sems):
    (
        hidden, hidden0, shard, old_logp, ref_logp, lengths, group_of, rewards, weights,
        info_own, info_y, info_line, info_z, send1, r1a, r1b, s2a, s2b, r2a, r2b,
        full_rows, terms, squares_own, squares, take, home, raw, states_out, terms_out,
    ) = refs
    swap_sem, iy, iz, del_sem, x_sem, r_sem, o_sem, own_info = sems
    x, y, z, q, half, s = net.x, net.y, net.z, net.q, net.half, net.s
    zm = z + 1 - 2 * half
    mate = net.at(core=0)
    info, length, group, reward, opening = own_info

    for k in range(1, NY):
        net.send(info_own, info_y.at[k], pair(iy, k), net.at(y=(y + k) % NY))
    own_rows = pl.ds(pl.multiple_of(q * COLS + y * WROWS, 16), WROWS)
    net.send(shard, weights.at[own_rows, pl.ds(COLS, COLS)], pair(swap_sem, 1), mate)
    line = info
    for k in range(1, NY):
        net.arrived(info_y.at[k], pair(iy, k))
        line += info_y[k]
    info_line[...] = line
    for k in range(1, NZ):
        net.send(info_line, info_z.at[k], pair(iz, k), net.at(z=(z + k) % NZ))

    lane = iota((8, 128), 1)
    col = iota((1, SLOTS), 1)
    spot = jnp.full((1, SLOTS), -1, jnp.int32)
    for i in range(4):
        p = col - i * LMAX
        spot = jnp.where((p >= 0) & (p < length[i]), opening[i] + p, spot)
    row = iota((SLOTS, 1), 0)
    turned = ((row // 4 % 8) * 8 + row // 32) * 4 + row % 4
    ratio = ref_logp[...] - old_logp[...]
    penalty = jnp.exp(ratio) - ratio - 1.0
    pen_col = jnp.sum(jnp.where(row == col, penalty, 0.0), axis=1, keepdims=True)
    swap = one_hot(turned == col)
    net.arrived(hidden0, pair(swap_sem, 0))

    total = line
    for k in range(1, NZ):
        net.arrived(info_z.at[k], pair(iz, k))
        total += info_z[k]

    first = (jnp.sum(jnp.where(lane < s, total, 0.0)) * 0.125).astype(jnp.int32)
    table1 = one_hot((((turned - first) & (SLOTS - 1))) == spot)
    table2 = one_hot((((row - first) & (SLOTS - 1))) == spot)
    lanes1, lanes2 = pl.ds(0, CUT), pl.ds(CUT, WIDE - CUT)

    def route_y(n, src, dst, lanes):
        dst[:, y] = src[:, y, :, lanes]
        for k in (4, 3, 5, 2, 6, 1, 7):
            t = (y + k) % NY
            net.send(src.at[:, t, :, lanes], dst.at[:, y], pair(del_sem, n, k), net.at(y=t))

    def wait_y(n, dst):
        for k in range(1, NY):
            net.arrived(dst.at[:, (y + NY - k) % NY], pair(del_sem, n, k))

    def route_z(n, src, dst, lanes):
        dst[z] = src[half, pl.ds(2 * q, 2), :, lanes]
        for k in (4, 3, 5, 2, 6, 1, 7):
            t = (z + k) % NZ
            net.send(src.at[t % 2, pl.ds(2 * (t // 2), 2), :, lanes], dst.at[z], pair(del_sem, n, k), net.at(z=t))

    def wait_z(n, dst):
        for k in range(1, NZ):
            net.arrived(dst.at[(z + NZ - k) % NZ], pair(del_sem, n, k))

    send1[0, :, :, :CUT] = tiles(picked(table1, hidden0[:, :CUT]))
    send1[1, :, :, :CUT] = tiles(picked(table1, hidden[:, :CUT]))
    route_y(0, send1, r1a, lanes1)

    mean = total * (1.0 / GROUP)
    mean_square = pltpu.roll(mean, 96, 1)
    spread = jnp.maximum(jnp.sqrt(mean_square - mean * mean), 1.0)
    adv_col = jnp.zeros((SLOTS, 1), F32)
    for i in range(4):
        value = jnp.where(lane == 64 + group[i], (reward[i] - mean) / spread, 0.0)
        adv_col = jnp.where(row // LMAX == i, jnp.sum(value) * 0.125, adv_col)
    term_lane = iota((SLOTS, TERMS), 1)
    own_terms = jnp.where(term_lane == 0, adv_col, jnp.where(term_lane == 1, pen_col, 0.0)).astype(BF16)
    send1[0, :, :, CUT:COLS] = tiles(picked(table2, hidden0[:, CUT:]))
    send1[1, :, :, CUT:COLS] = tiles(picked(table2, hidden[:, CUT:]))
    moved = tiles(picked(table2, own_terms))
    send1[0, :, :, COLS:] = moved
    send1[1, :, :, COLS:] = moved
    route_z(1, send1, r1b, lanes2)

    counts = total.astype(BF16)
    sender = iota((128, SLOTS), 0)
    natural = iota((128, SLOTS), 1) // 4
    swapped = (natural % 8) * 8 + natural // 8
    w = iota((TOK, 1), 0)
    same = w % 4 == col % 4

    def bounds(order):
        low = jnp.dot(counts, one_hot(sender < order), preferred_element_type=F32)[0:1]
        high = jnp.dot(counts, one_hot(sender <= order), preferred_element_type=F32)[0:1]
        return low, high

    def pick_table(limits, e):
        packed = ((w // 4) * SLOTS + ((2 * q + e) * NY + y) * 4 + w % 4).astype(F32)
        return one_hot((limits[0] <= packed) & (packed < limits[1]) & same)

    limits1, limits2 = bounds(natural), bounds(swapped)
    pick1 = [pick_table(limits1, e) for e in range(2)]
    pick2 = [pick_table(limits2, e) for e in range(2)]

    whole = pl.ds(0, CUT)
    wait_y(0, r1a)
    for c in range(2):
        s2a[c] = tiles(picked(swap, flat(r1a[c])))
    route_z(2, s2a, r2a, whole)
    wait_z(1, r1b)
    for e in range(2):
        s2b[e] = tiles(picked(swap, flat(r1b[:, e])))
    route_y(3, s2b, r2b, whole)

    wait_z(2, r2a)
    for e in range(2):
        full_rows[x, e * TOK : (e + 1) * TOK, :CUT] = picked(pick1[e], flat(r2a[:, e]))
    wait_y(3, r2b)
    for e in range(2):
        full_rows[x, e * TOK : (e + 1) * TOK, CUT:] = picked(pick2[e], flat(r2b[e, :, :, : COLS - CUT]))

    x_up, x_dn = net.at(x=(x + 1) % NX), net.at(x=(x + NX - 1) % NX)
    x_l, x_r, x_f = (x + NX - 1) % NX, (x + 1) % NX, (x + 2) % NX

    def part(xx, i):
        return full_rows.at[xx, pl.ds(i * TOK, TOK), :]

    def over(xx, i, way, slot):
        net.send(part(xx, i), part(xx, i), pair(x_sem, way, slot), (x_up, x_dn)[way])

    def down(xx, n, i):
        net.send(part(xx, i), raw.at[xx, pl.ds(i * TOK, TOK), :], pair(r_sem, n, i), mate)

    over(x, 0, 0, 0)
    over(x, 1, 1, 1)
    over(x, 1, 0, 1)
    over(x, 0, 1, 0)
    down(x, 0, 0)
    down(x, 0, 1)
    chosen = jnp.where(half == 0, pick2[0].astype(F32), pick2[1].astype(F32)).astype(BF16)
    terms[...] = picked(chosen, flat(r2b[half, :, :, COLS - CUT :]))
    net.send(terms, terms, pair(o_sem, 5), mate)
    terms_out[...] = terms[:, :2]

    square = [jnp.zeros((2 * TOK, 128), F32)]

    def add_squares(xx):
        wide = full_rows[xx].astype(F32)
        for t in range(COLS // 128):
            tile = wide[:, t * 128 : (t + 1) * 128]
            square[0] += tile * tile

    add_squares(x)
    net.arrived(part(x_l, 0), pair(x_sem, 0, 0))
    over(x_l, 0, 0, 2)
    net.arrived(part(x_r, 1), pair(x_sem, 1, 1))
    over(x_r, 1, 1, 2)
    down(x_l, 1, 0)
    down(x_r, 2, 1)
    net.arrived(part(x_l, 1), pair(x_sem, 0, 1))
    down(x_l, 1, 1)
    net.arrived(part(x_r, 0), pair(x_sem, 1, 0))
    down(x_r, 2, 0)
    add_squares(x_l)
    add_squares(x_r)
    net.arrived(part(x_f, 0), pair(x_sem, 0, 2))
    down(x_f, 3, 0)
    net.arrived(part(x_f, 1), pair(x_sem, 1, 2))
    down(x_f, 3, 1)
    add_squares(x_f)
    squares_own[...] = lax.dot_general(
        jnp.ones((8, 128), F32), square[0], (((1,), (1,)), ((), ())),
        precision=lax.Precision.HIGHEST, preferred_element_type=F32,
    )
    net.send(squares_own, squares.at[0], pair(o_sem, 0), mate)
    net.send(squares_own, squares.at[1], pair(o_sem, 1), net.at(z=zm, core=0))

    net.arrived(home, pair(o_sem, 4))
    net.arrived(take, pair(o_sem, 3))
    states_out[...] = (home[...] + take[...].astype(F32)).astype(BF16)
    net.finish()


SCRATCH = dict(
    info_own=((8, 128), F32),
    info_y=((NY, 8, 128), F32),
    info_line=((8, 128), F32),
    info_z=((NZ, 8, 128), F32),
    send1=((2, 8, 32, WIDE), BF16),
    r1a=((2, 8, 32, CUT), BF16),
    r1b=((8, 2, 32, CUT), BF16),
    s2a=((2, 8, 32, CUT), BF16),
    s2b=((2, 8, 32, CUT), BF16),
    r2a=((8, 2, 32, CUT), BF16),
    r2b=((2, 8, 32, CUT), BF16),
    full_rows=((NX, 2 * TOK, COLS), BF16),
    raw=((NX, 2 * TOK, COLS), BF16),
    terms=((TOK, TERMS), BF16),
    hidden0=((SLOTS, COLS), BF16),
    weights=((NQ * COLS, BOTH), BF16),
    scaled=((2 * TOK, NX * COLS), BF16),
    product=((2 * TOK, BOTH), F32),
    give=((2, TOK, COLS), BF16),
    take=((TOK, COLS), BF16),
    home=((TOK, COLS), F32),
    squares_own=((8, 2 * TOK), F32),
    squares=((2, 8, 2 * TOK), F32),
)
SEMAPHORES = dict(
    swap=(2,),
    iy=(8,),
    iz=(8,),
    deliver=(4, 8),
    pa=(2,),
    pf=(2,),
    pb=(2, 5),
    a2=(2, 5, 4),
    b2=(2, 3, 8),
    x=(2, 3),
    r=(4, 2),
    o=(6,),
)


def kernel(hidden, shard, gain, old_logp, ref_logp, lengths, group_of, rewards, states_out, terms_out, *rest):
    v = dict(zip(SCRATCH, rest))
    sem_refs = rest[len(SCRATCH) :]
    m = {n: (sem_refs[2 * i], sem_refs[2 * i + 1]) for i, n in enumerate(SEMAPHORES)}
    own_sem = sem_refs[-1]

    net = Links()
    y, z = net.y, net.z
    other = 1 - net.core
    barrier = pltpu.get_barrier_semaphore()
    partners = [net.at(y=(y + k) % NY) for k in range(1, NY)]
    partners += [net.at(z=(z + k) % NZ) for k in range(1, NZ)]
    partners += [net.at(x=(net.x + k) % NX) for k in range(1, NX)]
    partners += [net.at(core=other), net.at(z=z + 1 - 2 * net.half, core=other)]
    for dev in partners:
        pl.semaphore_signal(barrier, inc=1, device_id=dev, device_id_type=MESH)

    lane = iota((8, 128), 1)
    length = [lengths[i] for i in range(4)]
    group = [group_of[i] for i in range(4)]
    reward = [rewards[i].astype(F32) for i in range(4)]
    opening = [0 * length[0]]
    for i in range(3):
        opening.append(opening[-1] + length[i])
    info = jnp.where(lane == net.s, (opening[3] + length[3]).astype(F32), 0.0)
    for i in range(4):
        info += jnp.where(lane == 64 + group[i], reward[i], 0.0)
        info += jnp.where(lane == 96 + group[i], reward[i] * reward[i], 0.0)
    v["info_own"][...] = info
    pl.semaphore_wait(barrier, len(partners))

    @pl.when(net.core == 0)
    def _():
        product_core(
            Links(),
            (
                shard, gain, v["weights"], v["scaled"], v["raw"], v["product"], v["give"], v["take"], v["home"], v["squares"],
                hidden, v["hidden0"], v["terms"], states_out, terms_out,
            ),
            (m["swap"], m["pa"], m["pf"], m["pb"], m["a2"], m["b2"], m["r"], m["o"], own_sem),
        )

    @pl.when(net.core == 1)
    def _():
        names = (
            "info_own", "info_y", "info_line", "info_z", "send1", "r1a", "r1b", "s2a", "s2b", "r2a", "r2b",
            "full_rows", "terms", "squares_own", "squares", "take", "home", "raw",
        )
        token_core(
            Links(),
            (hidden, v["hidden0"], shard, old_logp, ref_logp, lengths, group_of, rewards, v["weights"])
            + tuple(v[n] for n in names)
            + (states_out, terms_out),
            (m["swap"], m["iy"], m["iz"], m["deliver"], m["x"], m["r"], m["o"], (info, length, group, reward, opening)),
        )


def shards(hidden, projection, norm_gain, old_logp, ref_logp, lengths, group_of, rewards):
    dma = pltpu.SemaphoreType.DMA
    vmem = pl.BlockSpec(memory_space=pltpu.VMEM)
    smem = pl.BlockSpec(memory_space=pltpu.SMEM)
    pairs = []
    for shape in SEMAPHORES.values():
        pairs += [dma(shape), dma(shape)]
    return pl.pallas_call(
        kernel,
        out_shape=(
            jax.ShapeDtypeStruct((TOK, COLS), BF16),
            jax.ShapeDtypeStruct((TOK, 2), BF16),
        ),
        in_specs=[vmem] * 5 + [smem] * 3,
        out_specs=(vmem, vmem),
        scratch_shapes=[pltpu.VMEM(*spec) for spec in SCRATCH.values()] + pairs + [dma((1,))],
        compiler_params=pltpu.CompilerParams(collective_id=0, has_side_effects=True),
    )(
        hidden,
        projection,
        norm_gain.reshape(1, D),
        old_logp.reshape(1, SLOTS),
        ref_logp.reshape(1, SLOTS),
        lengths,
        group_of,
        rewards,
    )


def solution(mesh):
    in_specs = (
        P("seq", ("sec", "tp")),
        P("seq", ("sec", "tp")),
        P(),
        P("seq"),
        P("seq"),
        P("seq"),
        P("seq"),
        P("seq"),
    )
    out_specs = (P("seq", ("sec", "tp")), P("seq", None))
    return jax.shard_map(shards, mesh=mesh, in_specs=in_specs, out_specs=out_specs, check_vma=False)
```

time: 127 us -> 70.4 us (0.55)
  Pallas kernels: 0 us -> 66.6 us
  waiting for transfers between devices: 45.8 us -> 0 us
  starting transfers between devices: 35.8 us -> 0 us
  between operations: 15.5 us -> 0.64 us
  other arithmetic: 12.9 us -> 0 us
  local copies, waits for them, and re-layouts: 9.92 us -> 2.95 us
  matrix products: 6.89 us -> 0 us
    pallas_call x0 -> x1, Pallas kernels: none -> 66.6 us  [shards(): pl.pallas_call(kernel, out_shape=(jax.ShapeDtypeStruct((TOK, COLS), BF16)...]
    all_to_all x4 -> x0, waiting for transfers between devices: 45.1 us -> none  [the longest x2 25.4 us: from_everyone(): return lax.all_to_all(copies, axis, split_axis=0, concat_axis=0, tiled=True)]
    all_to_all x4 -> x0, starting transfers between devices: 35.7 us -> none  [the longest x2 24.7 us: from_everyone(): return lax.all_to_all(copies, axis, split_axis=0, concat_axis=0, tiled=True)]
    dot_general x5 -> x0, matrix products: 6.89 us -> none  [the longest x1 4.76 us: refine(): jnp.dot(normed, lax.all_gather(projection, 'seq', axis=0, tiled=True), pr...]
    gather x9 -> x0, local copies, waits for them, and re-layouts: 5.5 us -> none  [the longest x2 1.34 us: deliver(): jnp.take(token_terms, source, axis=0)]
    gather x3 -> x0, other arithmetic: 3.13 us -> none  [the longest x1 3.12 us: deliver(): opening = jnp.take(finish - lengths, response)]
    select_n x8 -> x0, other arithmetic: 2.65 us -> none  [the longest x1 1.09 us: deliver(): jnp.where(filled[:, None], jnp.take(input_rows, source, axis=0), jnp.zero...]
    reduce_sum x5 -> x0, other arithmetic: 2.21 us -> none  [the longest x1 1.31 us: shards(): own_total = jnp.sum(lengths)]
  transfers between devices with their start and end apart: 5 -> 0, of which waited for: 4 -> 0; matrix products, arithmetic and copies ran while one was open for 20% -> 0% of each run, Pallas kernels for 0% -> 0%
where the time goes in v2:
time: 70.4 us; the launch traced here: 70.2 us
  Pallas kernels  66.6 us (95%)
  local copies, waits for them, and re-layouts  2.95 us (4%)
    pallas_call x1, Pallas kernels, shards(): pl.pallas_call(kernel, out_shape=(jax.ShapeDtypeStruct((TOK, COLS), BF16)...  66.6 us
    unnamed x1, local copies, waits for them, and re-layouts  1.6 us

profile of v2, /device:TPU:1, one launch (start us, length us, event | category | flops | bytes accessed | tf_op | source)
XLA Modules:
  0.0 70.2 jit_solution(2757859453315480249)
XLA Ops:
  0.6 66.6 %shard_map.95 = (bf16[128,640]{1,0:T(8,128)(2,1)}, bf16[128,2]{1,0:T(8,128)(2,1)}) custom-call(bf16[256,640]{1,0:T(8,128)(2,1)} %hidden.1, bf16[80,640]{1,0:T(8,128)(2,1)} %shard.1, f32[1,5120]{1,0:T(1,128)} %bitcast.3, f32[1,256]{1,0:T(1,128)} %bitcast.4, f32[1,256]{1,0:T(1,128)} %bitcast.5, s32[4]{0:T(128)} %lengths.1, s32[4]{0:T(128)} %group_of.1, s32[4]{0:T(128)} %rewards.1), custom_call_target="tpu_custom_call" | custom-call | tf_op jit(solution)/shard_map/pallas_call | solution.py:514
  67.2 1.4 %copy.10 = bf16[128,2]{0,1:T(2,128)(2,1)} copy(bf16[128,2]{1,0:T(8,128)(2,1)} %get-tuple-element.3) | data formatting | bytes 1024 | tf_op jit(solution)/shard_map/pallas_call | solution.py:514
  68.6 1.6 %copy.12 = bf16[128,640]{1,0:T(8,128)(2,1)} copy(bf16[128,640]{1,0:T(8,128)(2,1)} %get-tuple-element.6) | data formatting | bytes 327680

commit v3 on v2

--- a/solution.py
+++ b/solution.py
@@ -196,7 +196,7 @@
         g = gain[:, pl.ds(pl.multiple_of((2 * xx + half) * COLS, 128), COLS)]
         scaled[:, pl.ds(pl.multiple_of(xx * COLS, 128), COLS)] = (raw[xx].astype(F32) * g).astype(BF16)
     net.arrived(terms, pair(o_sem, 5))
-    terms_out[...] = terms[:, :2]
+    terms_out[...] = terms[:2, :]
     net.arrived(squares.at[0], pair(o_sem, 0))
     net.arrived(squares.at[1], pair(o_sem, 1))
     rate = lax.rsqrt((squares[0] + squares[1])[0:1] * (1.0 / D) + 1e-6)
@@ -363,9 +363,11 @@
     down(x, 0, 0)
     down(x, 0, 1)
     chosen = jnp.where(half == 0, pick2[0].astype(F32), pick2[1].astype(F32)).astype(BF16)
-    terms[...] = picked(chosen, flat(r2b[half, :, :, COLS - CUT :]))
+    terms[...] = lax.dot_general(
+        flat(r2b[half, :, :, COLS - CUT :]), chosen, (((0,), (1,)), ((), ())), preferred_element_type=F32
+    ).astype(BF16)
     net.send(terms, terms, pair(o_sem, 5), mate)
-    terms_out[...] = terms[:, :2]
+    terms_out[...] = terms[:2, :]
 
     square = [jnp.zeros((2 * TOK, 128), F32)]
 
@@ -420,7 +422,7 @@
     r2b=((2, 8, 32, CUT), BF16),
     full_rows=((NX, 2 * TOK, COLS), BF16),
     raw=((NX, 2 * TOK, COLS), BF16),
-    terms=((TOK, TERMS), BF16),
+    terms=((TERMS, TOK), BF16),
     hidden0=((SLOTS, COLS), BF16),
     weights=((NQ * COLS, BOTH), BF16),
     scaled=((2 * TOK, NX * COLS), BF16),
@@ -430,7 +432,13 @@
     home=((TOK, COLS), F32),
     squares_own=((8, 2 * TOK), F32),
     squares=((2, 8, 2 * TOK), F32),
+    hidden=((SLOTS, COLS), BF16),
+    shard=((WROWS, COLS), BF16),
+    gain=((1, D), F32),
+    old_logp=((1, SLOTS), F32),
+    ref_logp=((1, SLOTS), F32),
 )
+INPUTS = ["hidden", "shard", "gain", "old_logp", "ref_logp"]
 SEMAPHORES = dict(
     swap=(2,),
     iy=(8,),
@@ -447,11 +455,14 @@
 )
 
 
-def kernel(hidden, shard, gain, old_logp, ref_logp, lengths, group_of, rewards, states_out, terms_out, *rest):
+def kernel(*refs):
+    inputs, (states_out, terms_out), rest = refs[:8], refs[8:10], refs[10:]
     v = dict(zip(SCRATCH, rest))
     sem_refs = rest[len(SCRATCH) :]
     m = {n: (sem_refs[2 * i], sem_refs[2 * i + 1]) for i, n in enumerate(SEMAPHORES)}
-    own_sem = sem_refs[-1]
+    own_sem, in_sem, *scalars = sem_refs[2 * len(SEMAPHORES) :]
+    hidden, shard, gain, old_logp, ref_logp = (v[n] for n in INPUTS)
+    lengths, group_of, rewards = scalars
 
     net = Links()
     y, z = net.y, net.z
@@ -464,6 +475,13 @@
     for dev in partners:
         pl.semaphore_signal(barrier, inc=1, device_id=dev, device_id_type=MESH)
 
+    loads = []
+    for i, dst in enumerate([hidden, shard, gain, old_logp, ref_logp, lengths, group_of, rewards]):
+        loads.append(pltpu.make_async_copy(inputs[i], dst, in_sem.at[i]))
+    for i in (5, 6, 7, 0, 1, 2, 3, 4):
+        loads[i].start()
+    for i in (5, 6, 7, 0, 1, 2, 3, 4):
+        loads[i].wait()
     lane = iota((8, 128), 1)
     length = [lengths[i] for i in range(4)]
     group = [group_of[i] for i in range(4)]
@@ -504,22 +522,29 @@
         )
 
 
+def handed_on(states, terms, states_out, terms_out):
+    states_out[...] = states[...]
+    terms_out[...] = terms[...]
+
+
 def shards(hidden, projection, norm_gain, old_logp, ref_logp, lengths, group_of, rewards):
     dma = pltpu.SemaphoreType.DMA
     vmem = pl.BlockSpec(memory_space=pltpu.VMEM)
-    smem = pl.BlockSpec(memory_space=pltpu.SMEM)
+    anywhere = pl.BlockSpec(memory_space=pltpu.MemorySpace.HBM)
     pairs = []
     for shape in SEMAPHORES.values():
         pairs += [dma(shape), dma(shape)]
-    return pl.pallas_call(
+    states, terms = pl.pallas_call(
         kernel,
         out_shape=(
             jax.ShapeDtypeStruct((TOK, COLS), BF16),
-            jax.ShapeDtypeStruct((TOK, 2), BF16),
+            jax.ShapeDtypeStruct((2, TOK), BF16),
         ),
-        in_specs=[vmem] * 5 + [smem] * 3,
+        in_specs=[anywhere] * 8,
         out_specs=(vmem, vmem),
-        scratch_shapes=[pltpu.VMEM(*spec) for spec in SCRATCH.values()] + pairs + [dma((1,))],
+        scratch_shapes=[pltpu.VMEM(*spec) for spec in SCRATCH.values()] + pairs
+        + [dma((1,)), dma((8,))]
+        + [pltpu.SMEM((4,), jnp.int32)] * 3,
         compiler_params=pltpu.CompilerParams(collective_id=0, has_side_effects=True),
     )(
         hidden,
@@ -531,6 +556,13 @@
         group_of,
         rewards,
     )
+    states, terms = pl.pallas_call(
+        handed_on,
+        out_shape=(jax.ShapeDtypeStruct((TOK, COLS), BF16), jax.ShapeDtypeStruct((2, TOK), BF16)),
+        in_specs=[vmem] * 2,
+        out_specs=(vmem, vmem),
+    )(states, terms)
+    return states, terms.T
 
 
 def solution(mesh):

time: 70.4 us -> 68 us (0.966)
  local copies, waits for them, and re-layouts: 2.95 us -> 0 us
    pallas_call x0 -> x1, Pallas kernels: none -> 1.6 us  [shards(): pl.pallas_call(handed_on, out_shape=(jax.ShapeDtypeStruct((TOK, COLS), BF...]
    unnamed x1 -> x0, local copies, waits for them, and re-layouts: 1.6 us -> none
    pallas_call x1 -> x0, local copies, waits for them, and re-layouts: 1.35 us -> none  [shards(): pl.pallas_call(kernel, out_shape=(jax.ShapeDtypeStruct((TOK, COLS), BF16)...]
    pallas_call x1, Pallas kernels: 66.6 us -> 65.6 us  [shards(): pl.pallas_call(kernel, out_shape=(jax.ShapeDtypeStruct((TOK, COLS), BF16)...]
where the time goes in v3:
time: 68 us; the launch traced here: 67.8 us
  Pallas kernels  67.2 us (99%)
    pallas_call x1, Pallas kernels, shards(): pl.pallas_call(kernel, out_shape=(jax.ShapeDtypeStruct((TOK, COLS), BF16)...  65.6 us
    pallas_call x1, Pallas kernels, shards(): pl.pallas_call(handed_on, out_shape=(jax.ShapeDtypeStruct((TOK, COLS), BF...  1.6 us

profile of v3, /device:TPU:1, one launch (start us, length us, event | category | flops | bytes accessed | tf_op | source)
XLA Modules:
  0.0 67.8 jit_solution(14659943132549530552)
XLA Ops:
  0.6 65.6 %shard_map.95 = (bf16[128,640]{1,0:T(8,128)(2,1)}, bf16[2,128]{1,0:T(2,128)(2,1)}) custom-call(bf16[256,640]{1,0:T(8,128)(2,1)} %refs_0_.1, bf16[80,640]{1,0:T(8,128)(2,1)} %refs_1_.1, f32[1,5120]{1,0:T(1,128)} %bitcast.4, f32[1,256]{1,0:T(1,128)} %bitcast.5, f32[1,256]{1,0:T(1,128)} %bitcast.6, s32[4]{0:T(128)} %refs_5_.1, s32[4]{0:T(128)} %refs_6_.1, s32[4]{0:T(128)} %refs_7_.1), custom_call_target="tpu_custom_call" | custom-call | tf_op jit(solution)/shard_map/pallas_call | solution.py:537
  66.2 1.6 %shard_map.96 = (bf16[128,640]{1,0:T(8,128)(2,1)}, bf16[2,128]{1,0:T(2,128)(2,1)}) custom-call(bf16[128,640]{1,0:T(8,128)(2,1)} %get-tuple-element.6.states, bf16[2,128]{1,0:T(2,128)(2,1)} %get-tuple-element.7.terms), custom_call_target="tpu_custom_call" | custom-call | tf_op jit(solution)/shard_map/pallas_call | solution.py:559

commit v4 on v3

--- a/solution.py
+++ b/solution.py
@@ -24,10 +24,10 @@
 MESH = pl.DeviceIdType.MESH
 ORDER = (
     (2, 0, 1), (2, 1, 1), (3, 1, 0, 0), (3, 1, 1, 0), (0, 0), (0, 1), (2, 0, 2), (2, 1, 2),
-    (4, 1, 0, 0), (3, 2, 0, 0), (3, 2, 1, 0), (3, 1, 0, 3), (3, 1, 1, 3), (4, 1, 1, 7), (3, 1, 0, 1), (3, 1, 1, 1),
-    (4, 1, 0, 1), (2, 0, 3), (2, 1, 3), (1, 0), (1, 1), (3, 3, 0, 0), (3, 2, 0, 3), (3, 2, 1, 3),
-    (4, 1, 1, 6), (3, 2, 0, 1), (3, 2, 1, 1), (2, 0, 4), (2, 1, 4), (4, 1, 0, 2), (3, 1, 0, 2), (3, 1, 1, 2),
-    (3, 3, 1, 3), (4, 1, 1, 5), (3, 3, 0, 1), (3, 2, 1, 2), (3, 2, 0, 2), (4, 1, 0, 3), (3, 3, 1, 2), (4, 1, 1, 4),
+    (4, 1, 0, 0), (3, 2, 0, 0), (3, 2, 1, 0), (4, 1, 1, 7), (3, 1, 0, 3), (3, 1, 1, 3), (3, 1, 0, 1), (3, 1, 1, 1),
+    (4, 1, 0, 1), (2, 0, 3), (2, 1, 3), (1, 0), (1, 1), (3, 3, 0, 0), (4, 1, 1, 6), (3, 2, 0, 3),
+    (3, 2, 1, 3), (3, 2, 0, 1), (3, 2, 1, 1), (4, 1, 0, 2), (2, 0, 4), (2, 1, 4), (3, 1, 0, 2), (3, 1, 1, 2),
+    (3, 3, 1, 3), (4, 1, 1, 5), (3, 3, 0, 1), (3, 2, 1, 2), (3, 2, 0, 2), (4, 1, 0, 3), (4, 1, 1, 4), (3, 3, 1, 2),
 )
 
 
@@ -204,15 +204,23 @@
     away = pl.ds(pl.multiple_of((1 - half) * TOK, TOK), TOK)
     near = pl.ds(pl.multiple_of(half * TOK, TOK), TOK)
 
-    for c, kind in ((0, 3), (1, 4)):
+    def arrive(kind):
         for item in [w for w in waiting if w[0] == kind]:
             hops[kind](*item[1:])
-        cols = pl.ds(c * COLS, COLS)
+
+    def refine(c, start, width, slot):
+        cols, own_cols = pl.ds(c * COLS + start, width), pl.ds(start, width)
         part = jnp.dot(scaled[...], weights[:, cols], preferred_element_type=F32)
         kept = jnp.where(half == c, 1.0, 0.0)
-        product[:, cols] = part * scale + raw[x].astype(F32) * kept
-        give[c] = product[away, cols].astype(BF16)
-        net.send(give.at[c], take, pair(o_sem, 2 + c), net.at(z=zm, core=c))
+        product[:, cols] = part * scale + raw[x, :, own_cols].astype(F32) * kept
+        give[c, :, own_cols] = product[away, cols].astype(BF16)
+        net.send(give.at[c, :, own_cols], take.at[:, own_cols], pair(o_sem, slot), net.at(z=zm, core=c))
+
+    arrive(4)
+    refine(1, WCUT - COLS, BOTH - WCUT, 3)
+    arrive(3)
+    refine(1, 0, WCUT - COLS, 6)
+    refine(0, 0, COLS, 2)
     net.send(product.at[near, pl.ds(COLS, COLS)], home, pair(o_sem, 4), mate)
     net.arrived(take, pair(o_sem, 2))
     states_out[...] = (product[near, :COLS] + take[...].astype(F32)).astype(BF16)
@@ -403,7 +411,8 @@
     net.send(squares_own, squares.at[1], pair(o_sem, 1), net.at(z=zm, core=0))
 
     net.arrived(home, pair(o_sem, 4))
-    net.arrived(take, pair(o_sem, 3))
+    net.arrived(take.at[:, pl.ds(WCUT - COLS, BOTH - WCUT)], pair(o_sem, 3))
+    net.arrived(take.at[:, pl.ds(0, WCUT - COLS)], pair(o_sem, 6))
     states_out[...] = (home[...] + take[...].astype(F32)).astype(BF16)
     net.finish()
 
@@ -451,7 +460,7 @@
     b2=(2, 3, 8),
     x=(2, 3),
     r=(4, 2),
-    o=(6,),
+    o=(7,),
 )
 
 

time: 68 us -> 66.5 us (0.978); the launches traced: 67.8 us -> 65.4 us
  Pallas kernels: 67.2 us -> 64.8 us
    pallas_call x1, Pallas kernels: 65.6 us -> 63.2 us  [shards(): pl.pallas_call(kernel, out_shape=(jax.ShapeDtypeStruct((TOK, COLS), BF16)...]
where the time goes in v4:
time: 66.5 us; the launch traced here: 65.4 us
  Pallas kernels  64.8 us (97%)
    pallas_call x1, Pallas kernels, shards(): pl.pallas_call(kernel, out_shape=(jax.ShapeDtypeStruct((TOK, COLS), BF16)...  63.2 us
    pallas_call x1, Pallas kernels, shards(): pl.pallas_call(handed_on, out_shape=(jax.ShapeDtypeStruct((TOK, COLS), BF...  1.6 us

profile of v4, /device:TPU:1, one launch (start us, length us, event | category | flops | bytes accessed | tf_op | source)
XLA Modules:
  0.0 65.4 jit_solution(3886811890478255044)
XLA Ops:
  0.6 63.2 %shard_map.95 = (bf16[128,640]{1,0:T(8,128)(2,1)}, bf16[2,128]{1,0:T(2,128)(2,1)}) custom-call(bf16[256,640]{1,0:T(8,128)(2,1)} %refs_0_.1, bf16[80,640]{1,0:T(8,128)(2,1)} %refs_1_.1, f32[1,5120]{1,0:T(1,128)} %bitcast.4, f32[1,256]{1,0:T(1,128)} %bitcast.5, f32[1,256]{1,0:T(1,128)} %bitcast.6, s32[4]{0:T(128)} %refs_5_.1, s32[4]{0:T(128)} %refs_6_.1, s32[4]{0:T(128)} %refs_7_.1), custom_call_target="tpu_custom_call" | custom-call | tf_op jit(solution)/shard_map/pallas_call | solution.py:546
  63.8 1.6 %shard_map.96 = (bf16[128,640]{1,0:T(8,128)(2,1)}, bf16[2,128]{1,0:T(2,128)(2,1)}) custom-call(bf16[128,640]{1,0:T(8,128)(2,1)} %get-tuple-element.6.states, bf16[2,128]{1,0:T(2,128)(2,1)} %get-tuple-element.7.terms), custom_call_target="tpu_custom_call" | custom-call | tf_op jit(solution)/shard_map/pallas_call | solution.py:568

commit v5 on v4

--- a/solution.py
+++ b/solution.py
@@ -220,9 +220,11 @@
     refine(1, WCUT - COLS, BOTH - WCUT, 3)
     arrive(3)
     refine(1, 0, WCUT - COLS, 6)
-    refine(0, 0, COLS, 2)
+    refine(0, 0, 256, 2)
+    refine(0, 256, 384, 7)
     net.send(product.at[near, pl.ds(COLS, COLS)], home, pair(o_sem, 4), mate)
-    net.arrived(take, pair(o_sem, 2))
+    net.arrived(take.at[:, pl.ds(0, 256)], pair(o_sem, 2))
+    net.arrived(take.at[:, pl.ds(256, 384)], pair(o_sem, 7))
     states_out[...] = (product[near, :COLS] + take[...].astype(F32)).astype(BF16)
     net.finish()
 
@@ -460,7 +462,7 @@
     b2=(2, 3, 8),
     x=(2, 3),
     r=(4, 2),
-    o=(7,),
+    o=(8,),
 )
 
 

time: 66.5 us -> 66.6 us (level)
  no operation moved by 1% of the time
where the time goes in v5:
time: 66.6 us; the launch traced here: 65.5 us
  Pallas kernels  64.9 us (97%)
    pallas_call x1, Pallas kernels, shards(): pl.pallas_call(kernel, out_shape=(jax.ShapeDtypeStruct((TOK, COLS), BF16)...  63.3 us
    pallas_call x1, Pallas kernels, shards(): pl.pallas_call(handed_on, out_shape=(jax.ShapeDtypeStruct((TOK, COLS), BF...  1.6 us

profile of v5, /device:TPU:1, one launch (start us, length us, event | category | flops | bytes accessed | tf_op | source)
XLA Modules:
  0.0 65.5 jit_solution(4562953154063083892)
XLA Ops:
  0.6 63.3 %shard_map.95 = (bf16[128,640]{1,0:T(8,128)(2,1)}, bf16[2,128]{1,0:T(2,128)(2,1)}) custom-call(bf16[256,640]{1,0:T(8,128)(2,1)} %refs_0_.1, bf16[80,640]{1,0:T(8,128)(2,1)} %refs_1_.1, f32[1,5120]{1,0:T(1,128)} %bitcast.4, f32[1,256]{1,0:T(1,128)} %bitcast.5, f32[1,256]{1,0:T(1,128)} %bitcast.6, s32[4]{0:T(128)} %refs_5_.1, s32[4]{0:T(128)} %refs_6_.1, s32[4]{0:T(128)} %refs_7_.1), custom_call_target="tpu_custom_call" | custom-call | tf_op jit(solution)/shard_map/pallas_call | solution.py:548
  63.9 1.6 %shard_map.96 = (bf16[128,640]{1,0:T(8,128)(2,1)}, bf16[2,128]{1,0:T(2,128)(2,1)}) custom-call(bf16[128,640]{1,0:T(8,128)(2,1)} %get-tuple-element.6.states, bf16[2,128]{1,0:T(2,128)(2,1)} %get-tuple-element.7.terms), custom_call_target="tpu_custom_call" | custom-call | tf_op jit(solution)/shard_map/pallas_call | solution.py:570
